TPU v7x, 128 devices: a whole 4x4x4 slice. The times are simulated.
128 devices in a mesh: row: 16 (over y_hi, z, core), col: 8 (over x, y_lo).
Axes of the slice: x: 4, y: 4 (y_hi: 2, y_lo: 2; y = y_hi * 2 + y_lo), z: 4, core: 2. Of those that a mesh axis runs over, the one named last changes fastest.
Arguments:
- factor: bfloat16 [16, 1536, 6144], P(None, 'row'), may hold values from -0.078125 to 0.078125
- inverse_blocks: bfloat16 [4, 1536, 1536], P(None, 'row'), as said below
- right_side: float32 [16, 1536, 4096], P(None, 'row', 'col'), may hold values from -6 to 6
- shape_derivative: float32 [4, 1536, 4096], P(None, 'row', 'col')
Outputs:
- solved: float32 [4, 1536, 4096], P(None, 'row', 'col')
- trailing: float32 [12, 1536, 4096], P(None, 'row', 'col')
- sensitivity: float32 [4, 1536], P(None, 'row')
Inputs may be any that keep to these rules, and one draw needn't show every extreme that they name: inverse_blocks[k] is the inverse supplied for the diagonal block of step k.
All inputs are finite; a program needn't handle non-finite values.
Results may differ from a plain program's by a relative error of at most 0.0045.
Values may be sent and summed in bfloat16 or wider, within the bound.
No kernel may reach another device: no remote copies, remote signals or barrier semaphores. Data moves between devices by JAX's collectives and lax.ppermute only.
A program may use at most 128 MiB of HBM per device.

v0:
```python
import jax
import jax.numpy as jnp
from jax import lax
from jax.sharding import PartitionSpec as P


def local(factor, inverse_blocks, right_side, shape_derivative):
    step_count = inverse_blocks.shape[0]
    block_size = inverse_blocks.shape[2]
    solved_list = []
    accum = right_side
    for step in range(step_count):
        residual = accum[step]
        gathered = lax.all_gather(residual.astype(jnp.bfloat16), "row", axis=0, tiled=True)
        own_rows = jnp.dot(inverse_blocks[step], gathered, preferred_element_type=jnp.float32)
        spread = lax.all_gather(own_rows.astype(jnp.bfloat16), "row", axis=0, tiled=True)
        own_rows, spread = (own_rows, spread)
        solved_list.append(own_rows)
        lower = factor[step + 1 :, :, step * block_size : (step + 1) * block_size]
        update = jnp.einsum("bij,jq->biq", lower, spread, preferred_element_type=jnp.float32)
        accum = jnp.concatenate([accum[: step + 1], accum[step + 1 :] - update], axis=0)
    trailing = accum[step_count:]
    solved = jnp.stack(solved_list)
    partial_terms = jnp.sum(solved * shape_derivative, axis=2)
    sensitivity = lax.psum(partial_terms, "col")
    return (solved, trailing, sensitivity)


def solution(mesh):
    placed = (
        P(None, "row", None),
        P(None, "row", None),
        P(None, "row", "col"),
        P(None, "row", "col"),
    )
    return jax.shard_map(
        local,
        mesh=mesh,
        in_specs=placed,
        out_specs=(P(None, "row", "col"), P(None, "row", "col"), P(None, "row")),
        check_vma=False,
    )
```

profile of v0, /device:TPU:1, one launch (start us, length us, event | category | flops | bytes accessed | tf_op | source)
XLA Modules:
  0.0 424.7 jit_solution(16260220490646862225)
XLA Ops:
  7.2 1.6 slice.118
  8.9 51.9 %all-gather.21.cloned.1.call-done = bf16[1,1536,512]{2,1,0:T(8,128)(2,1)} async-done(((bf16[1,96,512]{2,1,0:T(8,128)(2,1)}), bf16[1,1536,512]{2,1,0:T(8,128)(2,1)}) %all-gather.21.cloned.1.call-update) | async-done | bytes 1572880 | tf_op jit(solution)/shard_map/all_gather | solution.py:14
  60.7 2.5 fusion.36
  63.4 45.3 %all-gather.13.cloned.1.call-done = bf16[1536,512]{1,0:T(8,128)(2,1)} async-done(((bf16[96,512]{1,0:T(8,128)(2,1)}), bf16[1536,512]{1,0:T(8,128)(2,1)}) %all-gather.13.cloned.1.call-update) | async-done | bytes 1572880 | tf_op jit(solution)/shard_map/all_gather | solution.py:16
  108.6 6.3 %bitcast_subtract_fusion = f32[15,96,512]{2,1,0:T(8,128)S(1)} fusion(f32[16,96,512]{2,1,0:T(8,128)} %param.6, bf16[16,96,6144]{2,1,0:T(8,128)(2,1)} %param.4, bf16[1536,512]{1,0:T(8,128)(2,1)} %all-gather.13.cloned.1.call-done), kind=kOutput, calls=%fused_computation.8 | convolution fusion | flops 2265661440 | bytes 11894784 | tf_op jit(solution)/shard_map/bij,jq->biq/dot_general | solution.py:20
  114.9 1.6 copy-done.4
  117.2 44.9 %all-gather.23.cloned.1.call-done = bf16[1,1536,512]{2,1,0:T(8,128)(2,1)} async-done(((bf16[1,96,512]{2,1,0:T(8,128)(2,1)}), bf16[1,1536,512]{2,1,0:T(8,128)(2,1)}) %all-gather.23.cloned.1.call-update) | async-done | bytes 1572880 | tf_op jit(solution)/shard_map/all_gather | solution.py:14
  162.1 2.4 bitcast_convert_fusion.2
  164.6 45.2 %all-gather.15.cloned.1.call-done = bf16[1536,512]{1,0:T(8,128)(2,1)} async-done(((bf16[96,512]{1,0:T(8,128)(2,1)}), bf16[1536,512]{1,0:T(8,128)(2,1)}) %all-gather.15.cloned.1.call-update) | async-done | bytes 1572880 | tf_op jit(solution)/shard_map/all_gather | solution.py:16
  209.9 5.9 %slice_subtract_fusion = f32[14,96,512]{2,1,0:T(8,128)S(1)} fusion(f32[15,96,512]{2,1,0:T(8,128)} %copy-done.4, bf16[16,96,6144]{2,1,0:T(8,128)(2,1)} %param.4, bf16[1536,512]{1,0:T(8,128)(2,1)} %all-gather.15.cloned.1.call-done), kind=kOutput, calls=%fused_computation.9 | convolution fusion | flops 2114617344 | bytes 11206656 | tf_op jit(solution)/shard_map/bij,jq->biq/dot_general | solution.py:20
  215.8 1.5 copy-done.3
  217.3 0.7 slice.116
  218.1 44.9 %all-gather.25.cloned.1.call-done = bf16[1,1536,512]{2,1,0:T(8,128)(2,1)} async-done(((bf16[1,96,512]{2,1,0:T(8,128)(2,1)}), bf16[1,1536,512]{2,1,0:T(8,128)(2,1)}) %all-gather.25.cloned.1.call-update) | async-done | bytes 1572880 | tf_op jit(solution)/shard_map/all_gather | solution.py:14
  263.0 2.4 bitcast_convert_fusion.1
  265.5 45.2 %all-gather.17.cloned.1.call-done = bf16[1536,512]{1,0:T(8,128)(2,1)} async-done(((bf16[96,512]{1,0:T(8,128)(2,1)}), bf16[1536,512]{1,0:T(8,128)(2,1)}) %all-gather.17.cloned.1.call-update) | async-done | bytes 1572880 | tf_op jit(solution)/shard_map/all_gather | solution.py:16
  310.7 5.5 %slice_subtract_fusion.1 = f32[13,96,512]{2,1,0:T(8,128)S(1)} fusion(f32[14,96,512]{2,1,0:T(8,128)} %copy-done.3, bf16[16,96,6144]{2,1,0:T(8,128)(2,1)} %param.4, bf16[1536,512]{1,0:T(8,128)(2,1)} %all-gather.17.cloned.1.call-done), kind=kOutput, calls=%fused_computation.10 | convolution fusion | flops 1963573248 | bytes 10518528 | tf_op jit(solution)/shard_map/bij,jq->biq/dot_general | solution.py:20
  316.2 1.5 copy-done.2
  317.7 0.7 slice.115
  318.4 44.9 %all-gather.27.cloned.1.call-done = bf16[1,1536,512]{2,1,0:T(8,128)(2,1)} async-done(((bf16[1,96,512]{2,1,0:T(8,128)(2,1)}), bf16[1,1536,512]{2,1,0:T(8,128)(2,1)}) %all-gather.27.cloned.1.call-update) | async-done | bytes 1572880 | tf_op jit(solution)/shard_map/all_gather | solution.py:14
  363.3 2.4 bitcast_convert_fusion
  365.8 1.0 multiply_reduce_fusion
  366.8 15.6 %psum.7 = f32[4,96]{1,0:T(4,128)} all-reduce(f32[4,96]{1,0:T(4,128)S(1)} %get-tuple-element.3), channel_id=1, replica_groups=mesh['row'=16,'col'=8] {'col'}, use_global_device_ids=true, to_apply=%region_1.0 | all-reduce | flops 384 | bytes 3072 | tf_op jit(solution)/shard_map/psum | solution.py:25
  382.3 28.9 %all-gather.19.cloned.1.call-done = bf16[1536,512]{1,0:T(8,128)(2,1)} async-done(((bf16[96,512]{1,0:T(8,128)(2,1)}), bf16[1536,512]{1,0:T(8,128)(2,1)}) %all-gather.19.cloned.1.call-update) | async-done | bytes 1572880 | tf_op jit(solution)/shard_map/all_gather | solution.py:16
  411.2 6.6 %slice_subtract_fusion.2 = f32[12,96,512]{2,1,0:T(8,128)} fusion(f32[13,96,512]{2,1,0:T(8,128)} %copy-done.2, bf16[16,96,6144]{2,1,0:T(8,128)(2,1)} %param.4, bf16[1536,512]{1,0:T(8,128)(2,1)} %all-gather.19.cloned.1.call-done), kind=kOutput, calls=%fused_computation.11 | convolution fusion | flops 1812529152 | bytes 9830400 | tf_op jit(solution)/shard_map/bij,jq->biq/dot_general | solution.py:20
  (24 shorter events, 1.1 us)
Async XLA Ops:
  7.2 53.6 %all-gather.21.cloned.1.call-start = ((), (), s32[]{:S(2)}) async-start(), calls=%async_computation.4 | async-start | bytes 1671168 | tf_op jit(solution)/shard_map/all_gather | solution.py:14
  8.8 99.8 %all-gather.13.cloned.1.call-start = ((), (), s32[]{:S(2)}) async-start(), calls=%async_computation | async-start | bytes 1671168 | tf_op jit(solution)/shard_map/all_gather | solution.py:16
  63.3 98.8 %copy-start = (bf16[4,96,1536]{2,1,0:T(8,128)(2,1)S(1)}, bf16[4,96,1536]{2,1,0:T(8,128)(2,1)}, u32[]{:S(2)}) copy-start(bf16[4,96,1536]{2,1,0:T(8,128)(2,1)} %param.5) | copy-start | bytes 3538948
  63.3 98.8 %all-gather.23.cloned.1.call-start = ((), (), s32[]{:S(2)}) async-start(), calls=%async_computation.5 | async-start | bytes 1671168 | tf_op jit(solution)/shard_map/all_gather | solution.py:14
  114.9 1.6 copy-start.4
  117.2 92.7 %all-gather.15.cloned.1.call-start = ((), (), s32[]{:S(2)}) async-start(), calls=%async_computation.1 | async-start | bytes 1671168 | tf_op jit(solution)/shard_map/all_gather | solution.py:16
  164.6 98.4 %all-gather.25.cloned.1.call-start = ((), (), s32[]{:S(2)}) async-start(), calls=%async_computation.6 | async-start | bytes 1671168 | tf_op jit(solution)/shard_map/all_gather | solution.py:14
  215.8 1.5 copy-start.3
  218.0 92.7 %all-gather.17.cloned.1.call-start = ((), (), s32[]{:S(2)}) async-start(), calls=%async_computation.2 | async-start | bytes 1671168 | tf_op jit(solution)/shard_map/all_gather | solution.py:16
  265.4 97.9 %all-gather.27.cloned.1.call-start = ((), (), s32[]{:S(2)}) async-start(), calls=%async_computation.7 | async-start | bytes 1671168 | tf_op jit(solution)/shard_map/all_gather | solution.py:14
  316.2 1.5 copy-start.2
  317.7 48.1 %copy-start.1 = (f32[4,96,512]{2,1,0:T(8,128)S(1)}, f32[4,96,512]{2,1,0:T(8,128)}, u32[]{:S(2)}) copy-start(f32[4,96,512]{2,1,0:T(8,128)} %param.7) | copy-start | bytes 2359300
  318.4 92.8 %all-gather.19.cloned.1.call-start = ((), (), s32[]{:S(2)}) async-start(), calls=%async_computation.3 | async-start | bytes 1671168 | tf_op jit(solution)/shard_map/all_gather | solution.py:16
Sparse Core Ops, SparseCore 0:
  11.0 49.6 all-gather.20
  63.8 44.7 all-gather.12
  117.3 44.7 all-gather.22
  165.0 44.7 all-gather.14
  218.1 44.7 all-gather.24
  265.9 44.7 all-gather.16
  318.5 44.7 all-gather.26
  366.4 44.7 all-gather.18
where the time goes:
time: 425 us
  waiting for transfers between devices  351 us (83%)
  matrix products  34.2 us (8%)
  blocking collectives  15.6 us (4%)
  between operations  14.2 us (3%)
  local copies, waits for them, and re-layouts  8.14 us (2%)
    all_gather x4, waiting for transfers between devices, local(): lax.all_gather(residual.astype(jnp.bfloat16), 'row', axis=0, tiled=True)  187 us
    all_gather x4, waiting for transfers between devices, local(): lax.all_gather(own_rows.astype(jnp.bfloat16), 'row', axis=0, tiled=True)  165 us
    dot_general x4, matrix products, local(): jnp.einsum('bij,jq->biq', lower, spread, preferred_element_type=jnp.float32)  24.3 us
    psum x1, blocking collectives, local(): sensitivity = lax.psum(partial_terms, 'col')  15.6 us
    dot_general x4, matrix products, local(): jnp.dot(inverse_blocks[step], gathered, preferred_element_type=jnp.float32)  9.85 us
  transfers between devices with their start and end apart: 8, of which 8 were waited for; matrix products, arithmetic and copies ran while one was open for 0% of the time, Pallas kernels for 0%

commit v1 on v0

--- a/solution.py
+++ b/solution.py
@@ -11,7 +11,12 @@
     accum = right_side
     for step in range(step_count):
         residual = accum[step]
-        gathered = lax.all_gather(residual.astype(jnp.bfloat16), "row", axis=0, tiled=True)
+        gathered = jnp.concatenate(
+            lax.all_to_all(
+                jnp.stack([residual.astype(jnp.bfloat16)] * lax.axis_size("row")), "row", 0, 0
+            ),
+            axis=0,
+        )
         own_rows = jnp.dot(inverse_blocks[step], gathered, preferred_element_type=jnp.float32)
         spread = lax.all_gather(own_rows.astype(jnp.bfloat16), "row", axis=0, tiled=True)
         own_rows, spread = (own_rows, spread)

time: 425 us -> 334 us (0.79)
  waiting for transfers between devices: 351 us -> 161 us
  blocking collectives: 15.6 us -> 127 us
  local copies, waits for them, and re-layouts: 8.14 us -> 1.66 us
  matrix products: 34.2 us -> 28.5 us
    all_gather x4 -> x0, waiting for transfers between devices: 187 us -> none  [local(): lax.all_gather(residual.astype(jnp.bfloat16), 'row', axis=0, tiled=True)]
    all_to_all x0 -> x4, blocking collectives: none -> 111 us  [local(): lax.all_to_all(jnp.stack([residual.astype(jnp.bfloat16)] * lax.axis_size(...]
    dot_general x4, matrix products: 9.85 us -> 4.13 us  [local(): jnp.dot(inverse_blocks[step], gathered, preferred_element_type=jnp.float32)]
    unnamed x10, local copies, waits for them, and re-layouts: 4.6 us -> 0.09 us
  transfers between devices with their start and end apart: 8 -> 4, of which waited for: 8 -> 4; matrix products, arithmetic and copies ran while one was open for 0% -> 0% of each run, Pallas kernels for 0% -> 0%
where the time goes in v1:
time: 334 us; the launch traced here: 333 us
  waiting for transfers between devices  161 us (48%)
  blocking collectives  127 us (38%)
  matrix products  28.5 us (9%)
  between operations  13.9 us (4%)
    all_gather x4, waiting for transfers between devices, local(): lax.all_gather(own_rows.astype(jnp.bfloat16), 'row', axis=0, tiled=True)  161 us
    all_to_all x4, blocking collectives, local(): lax.all_to_all(jnp.stack([residual.astype(jnp.bfloat16)] * lax.axis_size(...  111 us
    dot_general x4, matrix products, local(): jnp.einsum('bij,jq->biq', lower, spread, preferred_element_type=jnp.float32)  24.3 us
    psum x1, blocking collectives, local(): sensitivity = lax.psum(partial_terms, 'col')  16.3 us
  transfers between devices with their start and end apart: 4, of which 4 were waited for; matrix products, arithmetic and copies ran while one was open for 0% of the time, Pallas kernels for 0%

profile of v1, /device:TPU:1, one launch (start us, length us, event | category | flops | bytes accessed | tf_op | source)
XLA Modules:
  0.0 333.5 jit_solution(2946057854177174953)
XLA Ops:
  7.2 0.9 fusion.32
  8.2 0.1 stack.27
  8.3 31.8 %all_to_all.20 = bf16[16,96,512]{2,1,0:T(8,128)(2,1)S(1)} all-to-all(bf16[16,96,512]{2,1,0:T(8,128)(2,1)S(1)} %stack.27), channel_id=1, replica_groups=mesh['row'=16,'col'=8] {'row'}, dimensions={0} | all-to-all | bytes 3145728 | tf_op jit(solution)/shard_map/all_to_all | solution.py:15
  40.1 1.0 fusion.36
  41.2 44.3 %all-gather.5.cloned.1.call-done = bf16[1536,512]{1,0:T(8,128)(2,1)} async-done(((bf16[96,512]{1,0:T(8,128)(2,1)}), bf16[1536,512]{1,0:T(8,128)(2,1)}) %all-gather.5.cloned.1.call-update) | async-done | bytes 1572880 | tf_op jit(solution)/shard_map/all_gather | solution.py:21
  85.5 6.3 %bitcast_subtract_fusion = f32[15,96,512]{2,1,0:T(8,128)S(1)} fusion(f32[16,96,512]{2,1,0:T(8,128)} %param.6, bf16[16,96,6144]{2,1,0:T(8,128)(2,1)} %param.4, bf16[1536,512]{1,0:T(8,128)(2,1)} %all-gather.5.cloned.1.call-done), kind=kOutput, calls=%fused_computation.8 | convolution fusion | flops 2265661440 | bytes 11894784 | tf_op jit(solution)/shard_map/bij,jq->biq/dot_general | solution.py:25
  91.8 0.1 stack.30
  92.0 26.3 %all_to_all.21 = bf16[16,96,512]{2,1,0:T(8,128)(2,1)S(1)} all-to-all(bf16[16,96,512]{2,1,0:T(8,128)(2,1)S(1)} %stack.30), channel_id=1, replica_groups=mesh['row'=16,'col'=8] {'row'}, dimensions={0} | all-to-all | bytes 3145728 | tf_op jit(solution)/shard_map/all_to_all | solution.py:15
  118.3 1.0 bitcast_convert_fusion.2
  119.4 44.7 %all-gather.7.cloned.1.call-done = bf16[1536,512]{1,0:T(8,128)(2,1)} async-done(((bf16[96,512]{1,0:T(8,128)(2,1)}), bf16[1536,512]{1,0:T(8,128)(2,1)}) %all-gather.7.cloned.1.call-update) | async-done | bytes 1572880 | tf_op jit(solution)/shard_map/all_gather | solution.py:21
  164.1 5.9 %slice_subtract_fusion = f32[14,96,512]{2,1,0:T(8,128)S(1)} fusion(f32[15,96,512]{2,1,0:T(8,128)} %copy-done.4, bf16[16,96,6144]{2,1,0:T(8,128)(2,1)} %param.4, bf16[1536,512]{1,0:T(8,128)(2,1)} %all-gather.7.cloned.1.call-done), kind=kOutput, calls=%fused_computation.9 | convolution fusion | flops 2114617344 | bytes 11206656 | tf_op jit(solution)/shard_map/bij,jq->biq/dot_general | solution.py:25
  170.1 0.1 stack.33
  170.3 26.3 %all_to_all.22 = bf16[16,96,512]{2,1,0:T(8,128)(2,1)S(1)} all-to-all(bf16[16,96,512]{2,1,0:T(8,128)(2,1)S(1)} %stack.33), channel_id=1, replica_groups=mesh['row'=16,'col'=8] {'row'}, dimensions={0} | all-to-all | bytes 3145728 | tf_op jit(solution)/shard_map/all_to_all | solution.py:15
  196.6 1.0 bitcast_convert_fusion.1
  197.7 44.7 %all-gather.9.cloned.1.call-done = bf16[1536,512]{1,0:T(8,128)(2,1)} async-done(((bf16[96,512]{1,0:T(8,128)(2,1)}), bf16[1536,512]{1,0:T(8,128)(2,1)}) %all-gather.9.cloned.1.call-update) | async-done | bytes 1572880 | tf_op jit(solution)/shard_map/all_gather | solution.py:21
  242.4 5.5 %slice_subtract_fusion.1 = f32[13,96,512]{2,1,0:T(8,128)S(1)} fusion(f32[14,96,512]{2,1,0:T(8,128)} %copy-done.3, bf16[16,96,6144]{2,1,0:T(8,128)(2,1)} %param.4, bf16[1536,512]{1,0:T(8,128)(2,1)} %all-gather.9.cloned.1.call-done), kind=kOutput, calls=%fused_computation.10 | convolution fusion | flops 1963573248 | bytes 10518528 | tf_op jit(solution)/shard_map/bij,jq->biq/dot_general | solution.py:25
  248.0 0.1 stack.36
  248.1 26.3 %all_to_all.23 = bf16[16,96,512]{2,1,0:T(8,128)(2,1)S(1)} all-to-all(bf16[16,96,512]{2,1,0:T(8,128)(2,1)S(1)} %stack.36), channel_id=1, replica_groups=mesh['row'=16,'col'=8] {'row'}, dimensions={0} | all-to-all | bytes 3145728 | tf_op jit(solution)/shard_map/all_to_all | solution.py:15
  274.4 1.0 bitcast_convert_fusion
  275.5 0.1 copy-done.1
  275.6 1.0 multiply_reduce_fusion
  276.5 16.3 %psum.7 = f32[4,96]{1,0:T(4,128)} all-reduce(f32[4,96]{1,0:T(4,128)S(1)} %get-tuple-element.3), channel_id=1, replica_groups=mesh['row'=16,'col'=8] {'col'}, use_global_device_ids=true, to_apply=%region_1.0 | all-reduce | flops 384 | bytes 3072 | tf_op jit(solution)/shard_map/psum | solution.py:30
  292.9 27.5 %all-gather.11.cloned.1.call-done = bf16[1536,512]{1,0:T(8,128)(2,1)} async-done(((bf16[96,512]{1,0:T(8,128)(2,1)}), bf16[1536,512]{1,0:T(8,128)(2,1)}) %all-gather.11.cloned.1.call-update) | async-done | bytes 1572880 | tf_op jit(solution)/shard_map/all_gather | solution.py:21
  320.3 6.6 %slice_subtract_fusion.2 = f32[12,96,512]{2,1,0:T(8,128)} fusion(f32[13,96,512]{2,1,0:T(8,128)} %copy-done.2, bf16[16,96,6144]{2,1,0:T(8,128)(2,1)} %param.4, bf16[1536,512]{1,0:T(8,128)(2,1)} %all-gather.11.cloned.1.call-done), kind=kOutput, calls=%fused_computation.11 | convolution fusion | flops 1812529152 | bytes 9830400 | tf_op jit(solution)/shard_map/bij,jq->biq/dot_general | solution.py:25
  (20 shorter events, 0.3 us)
Async XLA Ops:
  7.2 78.3 %all-gather.5.cloned.1.call-start = ((), (), s32[]{:S(2)}) async-start(), calls=%async_computation.4 | async-start | bytes 1671168 | tf_op jit(solution)/shard_map/all_gather | solution.py:21
  8.3 31.8 %copy-start = (bf16[4,96,1536]{2,1,0:T(8,128)(2,1)S(1)}, bf16[4,96,1536]{2,1,0:T(8,128)(2,1)}, u32[]{:S(2)}) copy-start(bf16[4,96,1536]{2,1,0:T(8,128)(2,1)} %param.5) | copy-start | bytes 3538948
  41.2 123.0 %all-gather.7.cloned.1.call-start = ((), (), s32[]{:S(2)}) async-start(), calls=%async_computation.5 | async-start | bytes 1671168 | tf_op jit(solution)/shard_map/all_gather | solution.py:21
  91.8 26.5 %copy-start.4 = (f32[15,96,512]{2,1,0:T(8,128)}, f32[15,96,512]{2,1,0:T(8,128)S(1)}, u32[]{:S(2)}) copy-start(f32[15,96,512]{2,1,0:T(8,128)S(1)} %bitcast_subtract_fusion) | copy-start | bytes 8847364
  119.3 123.1 %all-gather.9.cloned.1.call-start = ((), (), s32[]{:S(2)}) async-start(), calls=%async_computation.6 | async-start | bytes 1671168 | tf_op jit(solution)/shard_map/all_gather | solution.py:21
  170.1 26.5 %copy-start.3 = (f32[14,96,512]{2,1,0:T(8,128)}, f32[14,96,512]{2,1,0:T(8,128)S(1)}, u32[]{:S(2)}) copy-start(f32[14,96,512]{2,1,0:T(8,128)S(1)} %slice_subtract_fusion) | copy-start | bytes 8257540
  197.6 122.7 %all-gather.11.cloned.1.call-start = ((), (), s32[]{:S(2)}) async-start(), calls=%async_computation.7 | async-start | bytes 1671168 | tf_op jit(solution)/shard_map/all_gather | solution.py:21
  247.9 26.5 %copy-start.2 = (f32[13,96,512]{2,1,0:T(8,128)}, f32[13,96,512]{2,1,0:T(8,128)S(1)}, u32[]{:S(2)}) copy-start(f32[13,96,512]{2,1,0:T(8,128)S(1)} %slice_subtract_fusion.1) | copy-start | bytes 7667716
  274.4 1.1 copy-start.1
Sparse Core Ops, SparseCore 0:
  41.3 44.1 all-gather.4
  119.4 44.6 all-gather.6
  197.7 44.6 all-gather.8
  275.6 44.6 all-gather.10
